TPU v7x, 512 devices: a whole 4x8x8 slice. The times are simulated.
512 devices in a mesh: pts: 128 (over z, y, core), rhs: 4 (over x).
Axes of the slice: x: 4, y: 8, z: 8, core: 2. Of those that a mesh axis runs over, the one named last changes fastest.
Arguments:
- points: bfloat16 [3, 524288], P(None, 'pts'), may hold values from -4 to 4
- values: bfloat16 [64, 524288], P('rhs', 'pts'), may hold values from -6 to 6
- leaf_basis: bfloat16 [32, 524288], P(None, 'pts'), may hold values from -0.75 to 0.75
- local_transfer: bfloat16 [16128, 32, 32], P('pts'), may hold values from -0.75 to 0.75
- upper_transfer: bfloat16 [254, 32, 32], replicated, may hold values from -0.75 to 0.75
- local_coupling: bfloat16 [16128, 4, 32, 32], P('pts'), may hold values from -0.5 to 0.5
- upper_coupling: bfloat16 [254, 4, 32, 32], replicated, may hold values from -0.5 to 0.5
- near_list: int32 [8192, 8], P('pts'), may hold values from -1 to 8191, as said below
- local_partners: int32 [16128, 4], P('pts'), may hold values from -1 to 8191, as said below
- upper_partners: int32 [254, 4], replicated, may hold values from -1 to 127, as said below
Outputs:
- product: bfloat16 [64, 524288], P('rhs', 'pts')
Inputs may be any that keep to these rules, and one draw needn't show every extreme that they name: `near_list`: entry 0 of row i is i itself; the other entries are -1 or distinct leaves at most 32 places from i. Some row has all 8 entries live, with offsets of both -32 and 32. `local_partners`: On every level some row holds offsets of both -n and n; some row has 4 live entries. `upper_partners`: A row of level 6 + k holds -1 or distinct other clusters of that level, given by their index on that level.
All inputs are finite; a program needn't handle non-finite values.
Results may differ from a plain program's by a relative error of at most 0.013.
Values may be sent and summed in bfloat16 or wider, within the bound.
No kernel may reach another device: no remote copies, remote signals or barrier semaphores. Data moves between devices by JAX's collectives and lax.ppermute only.
A program may use at most 64 MiB of HBM per device.

v0:
```python
import functools

import jax
import jax.numpy as jnp
from jax import lax
from jax.experimental import pallas as pl
from jax.experimental.pallas import tpu as pltpu
from jax.sharding import PartitionSpec as P

BF = jnp.bfloat16
F32 = jnp.float32
COLS = 16
RANK = 32
POINTS = 4096
HALF = POINTS // 2
GROUP = 128

LOCAL_BASE = (0, 16, 24, 28, 30, 31)
UPPER_BASE = (0, 32, 48, 56, 60, 62, 63)


def _dot(a, b, ca, cb):
    return lax.dot_general(a, b, (((ca,), (cb,)), ((), ())), preferred_element_type=F32)


def nn(a, b):
    return _dot(a, b, 1, 0)


def nt(a, b):
    return _dot(a, b, 1, 1)


def iota(shape, dim):
    return lax.broadcasted_iota(jnp.int32, shape, dim)


def ones_where(cond):
    return jnp.where(cond, F32(1), F32(0)).astype(BF)


def pair_mask():
    shape = (128, 256)
    return ones_where(iota(shape, 0) // 32 == iota(shape, 1) // 64)


def spread_mask():
    shape = (128, 512)
    row, col = iota(shape, 0), iota(shape, 1)
    return ones_where((row // 32 == col // 128) & (row % 32 == col % 32))


def tile_rows(x):
    return jnp.concatenate([x, x, x, x], axis=0)


def to_chunks(matrix_ref, chunk_ref, count, chunks):
    keep = ones_where(iota((128, count), 1) % 4 == iota((128, count), 0) // 32)
    pick = ones_where(iota((chunks, count), 1) // 4 == iota((chunks, count), 0))
    for r in range(RANK):
        part = tile_rows(matrix_ref[r]) * keep
        chunk_ref[pl.ds(r, chunks, stride=RANK), :] = nt(pick, part)


def chunk_of(ref, index):
    return ref[index * RANK : (index + 1) * RANK, :].astype(BF)


def up_kernel(
    place_ref, values_ref, points_ref, basis_ref, transfer_ref,
    first_ref, second_ref, aug_ref, root_ref, chunks_ref, scratch_ref,
):
    mask = pair_mask()
    to_chunks(transfer_ref, scratch_ref, 126, 32)
    blocks = [chunk_of(scratch_ref, i) for i in range(32)]
    for i in range(32):
        chunks_ref[i] = blocks[i]
    upward = []
    for g in range(16):
        lanes = slice(g * 256, (g + 1) * 256)
        weights = tile_rows(basis_ref[:, lanes]) * mask
        upward.append(nt(values_ref[:, lanes], weights).astype(BF))
    for base, below in ((16, 0), (24, 16), (28, 24), (30, 28)):
        for j in range((base - below) // 2):
            c = below + 2 * j
            weights = tile_rows(jnp.concatenate([blocks[c], blocks[c + 1]], axis=1)) * mask
            children = jnp.concatenate([upward[c], upward[c + 1]], axis=1)
            upward.append(nt(children, weights).astype(BF))
    upward.append(nt(upward[30], tile_rows(blocks[30]) * mask[:, :128]).astype(BF))
    root = nt(upward[31], tile_rows(blocks[31])).astype(BF).astype(F32)
    shape = (COLS, 128)
    root = jnp.where(iota(shape, 0) // 4 == iota(shape, 1) // 32, root, 0.0)
    root = root[:8] + root[8:]
    root = jnp.concatenate([root[:4] + root[4:]] * 2, axis=0).astype(BF)
    for i in range(64):
        root_ref[i * 8 : (i + 1) * 8, :] = root

    coords = points_ref[...].astype(F32)
    square = coords * coords
    square = square[0:1] + square[1:2] + square[2:3]
    high = square.astype(BF).astype(F32)
    middle = (square - high).astype(BF).astype(F32)
    low = (square - high - middle).astype(BF).astype(F32)
    row = iota((16, POINTS), 0)
    aug = jnp.where(row == 0, coords[0:1], jnp.where(row == 1, coords[1:2], coords[2:3]))
    aug = jnp.where(row < 3, aug, jnp.where(row < 6, 1.0, jnp.where(row == 6, -high, jnp.where(row == 7, -middle, -low))))
    aug = jnp.where(row < 9, aug, 0.0).astype(BF)
    aug_ref[...] = aug

    odd = lax.rem(place_ref[0], 2)
    for ref, start in ((first_ref, (1 - odd) * HALF), (second_ref, odd * HALF)):
        start = pl.multiple_of(start, HALF)
        ref[:, 0:HALF] = values_ref[:, pl.ds(start, HALF)]
        ref[:, HALF : 2 * HALF] = aug_ref[:, pl.ds(start, HALF)]
        for i in range(32):
            ref[:, 2 * HALF + i * 128 : 2 * HALF + (i + 1) * 128] = upward[i]


def operator_kernel(
    place_ref, partners_ref, transfer_ref, coupling_ref, order_ref,
    out_ref, blocks_ref, near_ref, spread_ref, weights_ref,
):
    del order_ref
    place = place_ref[0]
    mask = pair_mask()
    to_chunks(transfer_ref, blocks_ref, 254, 64)
    level = iota((8, 254), 0)
    mine = 256 - (256 >> level) + (place >> level)
    chosen = ones_where((iota((8, 254), 1) == mine) & (level < 7))
    for r in range(RANK):
        part = jnp.concatenate([coupling_ref[f, r] for f in range(4)], axis=0)
        near_ref[pl.ds(r, 8, stride=RANK), :] = nt(chosen, part)
    lane_group = iota((RANK, 128), 1) // 32
    chain = ones_where(iota((RANK, 128), 0) == iota((RANK, 128), 1) % 32)
    direct = []
    for k in range(7):
        direct.append(nn(chain[:, :RANK], chunk_of(near_ref, k)).astype(BF))
        if k < 6:
            own = place >> k
            at = pl.multiple_of((UPPER_BASE[k] + (own >> 2)) * RANK, RANK)
            block = blocks_ref[pl.ds(at, RANK), :]
            block = jnp.where(lane_group == (own & 3), block, 0.0).astype(BF)
            chain = nt(chain, tile_rows(block)).astype(BF)
    spread_ref[...] = nn(jnp.concatenate(direct, axis=0), spread_mask())
    weights_ref[...] = jnp.zeros_like(weights_ref)
    for k in range(7):
        row = 256 - (256 >> k) + (place >> k)
        for f in range(4):
            partner = partners_ref[f, row]
            found = jnp.maximum(partner, 0)
            at = pl.multiple_of((UPPER_BASE[k] + (found >> 2)) * RANK, RANK)
            group = jnp.where(partner < 0, -1, found & 3)
            term = spread_ref[k * RANK : (k + 1) * RANK, f * 128 : (f + 1) * 128]
            old = weights_ref[pl.ds(at, RANK), :]
            weights_ref[pl.ds(at, RANK), :] = old + jnp.where(lane_group == group, term, 0.0)
    held = {63: chunk_of(weights_ref, 63)}
    step = nn(held[63], tile_rows(chunk_of(blocks_ref, 62)) * mask[:, :128])
    held[62] = (weights_ref[62 * RANK : 63 * RANK, :] + step).astype(BF)
    for k in (4, 3, 2, 1, 0):
        for j in range((UPPER_BASE[k + 1] - UPPER_BASE[k]) // 2):
            c = UPPER_BASE[k] + 2 * j
            pair = jnp.concatenate([chunk_of(blocks_ref, c), chunk_of(blocks_ref, c + 1)], axis=1)
            step = nn(held[UPPER_BASE[k + 1] + j], tile_rows(pair) * mask)
            for h in range(2):
                total = weights_ref[(c + h) * RANK : (c + h + 1) * RANK, :]
                held[c + h] = (total + step[:, h * 128 : (h + 1) * 128]).astype(BF)
    for c in range(32):
        out_ref[c] = held[c]


def near_kernel(
    place_ref, list_ref, values_ref, aug_ref, first_ref, second_ref,
    near_ref, low_ref, high_ref, target_ref,
):
    place = place_ref[0]
    odd = lax.rem(place, 2)
    shape = (128, 512)
    row, col = iota(shape, 0), iota(shape, 1)
    part = col // 128
    lane = col % 128
    copy = ones_where((lane // 64 == part % 2) & (row == lane % 64 + 64 * (part // 2)))

    def stage(ref, first_leaf, chunks, value_at, aug_source, aug_at):
        rows = []
        for i in range(chunks):
            rows.append(ref[:, value_at + i * 128 : value_at + (i + 1) * 128])
            rows.append(aug_source[:, aug_at + i * 128 : aug_at + (i + 1) * 128])
        out = nn(jnp.concatenate(rows, axis=0), copy).astype(BF)
        for i in range(chunks):
            for h in range(2):
                block = out[i * 32 : (i + 1) * 32, h * 256 : (h + 1) * 256]
                low_ref[first_leaf + 2 * i + h] = block[:, :128]
                high_ref[first_leaf + 2 * i + h] = block[:, 128:]

    stage(values_ref, 32, 16, 0, aug_ref, 0)
    stage(values_ref, 64, 16, HALF, aug_ref, HALF)
    stage(first_ref, pl.multiple_of((1 - odd) * 96, 32), 16, 0, first_ref, HALF)
    stage(second_ref, pl.multiple_of(odd * 96, 32), 16, 0, second_ref, HALF)
    low_ref[128] = jnp.zeros((32, 128), BF)
    high_ref[128] = jnp.zeros((32, 128), BF)

    row, col = iota((16, 16), 0), iota((16, 16), 1)
    swap = jnp.where(
        (row < 3) & (row == col), 2.0,
        jnp.where((row >= 3) & (col >= 3) & (row < 9) & (col < 9) & ((row + 3 == col) | (row == col + 3)), 1.0, 0.0),
    ).astype(BF)
    for i in range(32):
        lanes = slice(i * 128, (i + 1) * 128)
        target_ref[lanes, :] = _dot(aug_ref[:, lanes], swap, 0, 0).astype(BF)

    base = place * 64 - 32

    def pair(m, carry):
        results = []
        for h in range(2):
            leaf = 2 * m + h
            columns = []
            for f in range(0, 8, 2):
                left, right = list_ref[f, leaf], list_ref[f + 1, leaf]
                left = jnp.where(left < 0, 128, left - base)
                right = jnp.where(right < 0, 128, right - base)
                columns.append(low_ref[left] + high_ref[right])
            stack = jnp.concatenate(columns, axis=1)
            targets = target_ref[pl.ds(pl.multiple_of(leaf * 64, 64), 64), :]
            kernel = jnp.exp(nn(targets, stack[16:])).astype(BF)
            results.append(nt(stack[:16], kernel))
        near_ref[:, pl.ds(pl.multiple_of(m * 128, 128), 128)] = jnp.concatenate(results, axis=1)
        return carry

    lax.fori_loop(0, 32, pair, 0, unroll=2)


def far_kernel(
    place_ref, partners_ref, coupling_ref, chunks_ref, basis_ref, near_ref, own_ref, first_ref, second_ref,
    base_ref, basis_out_ref, blocks_ref, spread_ref, coupled_ref,
):
    place = place_ref[0]
    odd = lax.rem(place, 2)
    same = ones_where(iota((128, 126), 0) == iota((128, 126), 1))
    for r in range(RANK):
        part = jnp.concatenate([coupling_ref[f, r] for f in range(4)], axis=0)
        blocks_ref[pl.ds(r, 128, stride=RANK), :] = nt(same, part)
    spread = spread_mask()
    for ref, first in ((own_ref, 128), (first_ref, (1 - odd) * 256), (second_ref, odd * 256)):
        rows = [ref[:, POINTS + i * 128 : POINTS + (i + 1) * 128] for i in range(32)]
        rows = jnp.concatenate(rows, axis=0)
        out = nn(rows, spread).astype(BF)
        for i in range(32):
            for j in range(4):
                block = out[i * COLS : (i + 1) * COLS, j * 128 : (j + 1) * 128]
                spread_ref[first + 4 * i + j] = block
    spread_ref[384] = jnp.zeros((COLS, 128), BF)

    group = iota((COLS, 128), 1) // 32
    slot_masks = [ones_where(group == f) for f in range(4)]
    zero = jnp.zeros((RANK, 128), BF)
    nothing = jnp.zeros((COLS, 128), BF)

    def couple(chunk, height, live):
        shift = 6 - height
        offset = 128 - (128 >> height)
        lefts, rights = [], []
        for j in range(4):
            if j >= live:
                lefts.append(nothing)
                rights.append(jnp.concatenate([zero] * 4, axis=1))
                continue
            total = nothing
            for f in range(4):
                partner = partners_ref[f, chunk * 4 + j]
                relative = partner - ((place - 1) << shift)
                at = ((relative >> shift) << 7) + offset + (relative & ((1 << shift) - 1))
                at = jnp.where(partner < 0, 384, at)
                total = total + spread_ref[at] * slot_masks[f]
            lefts.append(total)
            block = blocks_ref[pl.ds(pl.multiple_of((chunk * 4 + j) * RANK, RANK), RANK), :].astype(BF)
            rights.append(jnp.concatenate([zero] * j + [block] + [zero] * (3 - j), axis=1))
        result = nt(jnp.concatenate(lefts, axis=1), jnp.concatenate(rights, axis=0))
        coupled_ref[pl.ds(pl.multiple_of(chunk * COLS, COLS), COLS), :] = result

    for height in range(6):
        first = LOCAL_BASE[height]
        count = 16 >> height if height < 5 else 1
        if count >= 4:
            lax.fori_loop(0, count, lambda i, c, f=first, h=height: (couple(f + i, h, 4), c)[1], 0, unroll=2)
        else:
            for i in range(count):
                couple(first + i, height, 4 if height < 5 else 2)

    mask = pair_mask()
    pad = jnp.zeros((RANK, 128), F32)

    def coupled(c):
        return coupled_ref[c * COLS : (c + 1) * COLS, :]

    held = {31: jnp.concatenate([coupled(31).astype(BF), chunks_ref[31]], axis=0)}
    step = nn(held[31], tile_rows(chunks_ref[30]) * mask[:, :128])
    held[30] = (step + jnp.concatenate([coupled(30), pad], axis=0)).astype(BF)
    for height in (3, 2, 1, 0):
        for j in range((LOCAL_BASE[height + 1] - LOCAL_BASE[height]) // 2):
            c = LOCAL_BASE[height] + 2 * j
            pair = jnp.concatenate([chunks_ref[c], chunks_ref[c + 1]], axis=1)
            step = nn(held[LOCAL_BASE[height + 1] + j], tile_rows(pair) * mask)
            for h in range(2):
                extra = jnp.concatenate([coupled(c + h), pad], axis=0)
                held[c + h] = (step[:, h * 128 : (h + 1) * 128] + extra).astype(BF)
    for g in range(16):
        lanes = slice(g * 256, (g + 1) * 256)
        out = nn(held[g], tile_rows(basis_ref[:, lanes]) * mask)
        base_ref[:, lanes] = near_ref[:, lanes] + out[:COLS]
        basis_out_ref[:, lanes] = out[COLS:].astype(BF)


def final_kernel(roots_ref, operator_ref, basis_ref, base_ref, out_ref):
    roots = roots_ref[...].astype(F32)
    roots = roots.reshape(32, COLS, 128)
    shape = (32, COLS, 128)
    device, column = iota(shape, 2) // 32, iota(shape, 1) // 4
    total = jnp.where(device == column, roots, 0.0)
    for d in range(1, 4):
        moved = pltpu.roll(pltpu.roll(roots, COLS - 4 * d, 1), 32 * d, 2)
        total = jnp.where(device == (column + d) % 4, moved, total)
    total = total.astype(BF)
    left = jnp.concatenate([total[i] for i in range(32)], axis=1)
    right = jnp.concatenate([operator_ref[i] for i in range(32)], axis=1)
    expansion = nt(left, right).astype(BF)
    for g in range(8):
        lanes = slice(g * 512, (g + 1) * 512)
        out_ref[:, lanes] = (base_ref[:, lanes] + nn(expansion, basis_ref[:, lanes])).astype(BF)


SMEM = pl.BlockSpec(memory_space=pltpu.SMEM)
VMEM = pl.BlockSpec(memory_space=pltpu.VMEM)
ANY = pl.BlockSpec(memory_space=pl.ANY)
SCRATCH = pltpu.VMEM


def call(kernel, ins, outs, scratch, name, interpret=False):
    return pl.pallas_call(
        kernel,
        in_specs=ins,
        out_specs=[VMEM] * len(outs),
        out_shape=[jax.ShapeDtypeStruct(s, d) for s, d in outs],
        scratch_shapes=scratch,
        compiler_params=pltpu.CompilerParams(vmem_limit_bytes=48 * 1024 * 1024),
        name=name,
        interpret=interpret,
    )


def kernels(interpret=False):
    up = call(
        up_kernel,
        [SMEM, VMEM, VMEM, VMEM, VMEM],
        [
            ((COLS, 2 * POINTS), BF),
            ((COLS, 2 * POINTS), BF),
            ((16, POINTS), BF),
            ((4 * GROUP, 128), BF),
            ((32, RANK, 128), BF),
        ],
        [SCRATCH((32 * RANK, 128), F32)],
        "up",
        interpret,
    )
    operator = call(
        operator_kernel,
        [SMEM, SMEM, VMEM, VMEM, ANY],
        [((32, RANK, 128), BF)],
        [
            SCRATCH((64 * RANK, 128), F32),
            SCRATCH((8 * RANK, 128), F32),
            SCRATCH((7 * RANK, 512), F32),
            SCRATCH((64 * RANK, 128), F32),
        ],
        "operator",
        interpret,
    )
    near = call(
        near_kernel,
        [SMEM, SMEM, VMEM, VMEM, VMEM, VMEM],
        [((COLS, POINTS), F32)],
        [SCRATCH((129, 32, 128), BF), SCRATCH((129, 32, 128), BF), SCRATCH((POINTS, 16), BF)],
        "near",
        interpret,
    )
    far = call(
        far_kernel,
        [SMEM, SMEM, VMEM, VMEM, VMEM, VMEM, VMEM, VMEM, VMEM],
        [((COLS, POINTS), F32), ((RANK, POINTS), BF)],
        [SCRATCH((128 * RANK, 128), F32), SCRATCH((385, COLS, 128), BF), SCRATCH((32 * COLS, 128), F32)],
        "far",
        interpret,
    )
    final = call(final_kernel, [VMEM] * 4, [((COLS, POINTS), BF)], [], "final", interpret)
    return up, operator, near, far, final


def shards(
    points, values, leaf_basis, local_transfer, upper_transfer, local_coupling, upper_coupling,
    near_list, local_partners, upper_partners,
):
    up, operator, near, far, final = kernels()
    place = lax.axis_index("pts").astype(jnp.int32).reshape(1)
    local_t = jnp.transpose(local_transfer, (1, 2, 0))
    upper_t = jnp.transpose(upper_transfer, (1, 2, 0))
    local_c = jnp.transpose(local_coupling, (1, 2, 3, 0))
    upper_c = jnp.transpose(upper_coupling, (1, 2, 3, 0))
    first, second, aug, root, chunks = up(place, values, points, leaf_basis, local_t)
    roots = lax.all_to_all(root.reshape(GROUP, 4, 128), "pts", 0, 0, tiled=True)
    inside = [(i, i ^ 1) for i in range(GROUP)]
    across = [(i, ((i + 1) ^ 1) - 1) for i in range(1, GROUP - 1)]
    first_in = lax.ppermute(first, "pts", inside)
    second_in = lax.ppermute(second, "pts", across)
    (op,) = operator(place, upper_partners.T, upper_t, upper_c, chunks)
    (near_field,) = near(place, near_list.T, values, aug, first_in, second_in)
    base, basis = far(place, local_partners.T, local_c, chunks, leaf_basis, near_field, first, first_in, second_in)
    (out,) = final(roots.reshape(4 * GROUP, 128), op, basis, base)
    return out


def solution(mesh):
    placed = (
        P(None, "pts"),
        P("rhs", "pts"),
        P(None, "pts"),
        P("pts", None, None),
        P(),
        P("pts", None, None, None),
        P(),
        P("pts", None),
        P("pts", None),
        P(),
    )
    return jax.shard_map(
        shards, mesh=mesh, in_specs=placed, out_specs=P("rhs", "pts"), check_vma=False
    )
```

profile of v0, /device:TPU:1, one launch (start us, length us, event | category | flops | bytes accessed | tf_op | source)
XLA Modules:
  0.0 55.6 jit_solution(9987021730303265804)
XLA Ops:
  0.0 0.0 copy-start.10
  0.0 0.0 copy-start.1
  0.0 1.0 %copy-done.1 = bf16[32,4096]{1,0:T(8,128)(2,1)S(1)} copy-done((bf16[32,4096]{1,0:T(8,128)(2,1)S(1)}, bf16[32,4096]{1,0:T(8,128)(2,1)}, u32[]{:S(2)}) %copy-start.1) | copy-done | bytes 262168
  1.0 0.0 copy-start.5
  1.0 0.9 %copy-done.5 = bf16[16,4096]{1,0:T(8,128)(2,1)S(1)} copy-done((bf16[16,4096]{1,0:T(8,128)(2,1)S(1)}, bf16[16,4096]{1,0:T(8,128)(2,1)}, u32[]{:S(2)}) %copy-start.5) | copy-done | bytes 131096
  1.9 0.0 copy-start.7
  1.9 0.9 %copy-done.7 = bf16[126,32,32]{0,2,1:T(8,128)(2,1)S(1)} copy-done((bf16[126,32,32]{0,2,1:T(8,128)(2,1)S(1)}, bf16[126,32,32]{0,2,1:T(8,128)(2,1)}, u32[]{:S(2)}) %copy-start.7) | copy-done | bytes 258072
  2.8 0.0 copy-start.8
  2.8 0.8 %copy-done.8 = bf16[3,4096]{1,0:T(4,128)(2,1)S(1)} copy-done((bf16[3,4096]{1,0:T(4,128)(2,1)S(1)}, bf16[3,4096]{1,0:T(4,128)(2,1)}, u32[]{:S(2)}) %copy-start.8) | copy-done | bytes 24600
  3.6 0.0 copy-start.6
  3.6 2.6 %up.1 = (bf16[16,8192]{1,0:T(8,128)(2,1)S(1)}, bf16[16,8192]{1,0:T(8,128)(2,1)S(1)}, bf16[16,4096]{1,0:T(8,128)(2,1)S(1)}, bf16[512,128]{1,0:T(8,128)(2,1)}, bf16[32,32,128]{2,1,0:T(8,128)(2,1)S(1)}) custom-call(s32[1]{0:T(128)} %bitcast.place_ref, bf16[16,4096]{1,0:T(8,128)(2,1)S(1)} %copy-done.5, bf16[3,4096]{1,0:T(4,128)(2,1)S(1)} %copy-done.8, ...), custom_call_target="tpu_custom_call" | custom-call | tf_op jit(solution)/shard_map/up/pallas_call | solution.py:409
  6.2 8.7 %collective-permute-start = (bf16[16,8192]{1,0:T(8,128)(2,1)S(1)}, bf16[16,8192]{1,0:T(8,128)(2,1)S(1)}, u32[]{:S(2)}, u32[]{:S(2)}) collective-permute-start(bf16[16,8192]{1,0:T(8,128)(2,1)S(1)} %get-tuple-element.15.own_ref), channel_id=1, source_target_pairs={{0,4},{4,0},{8,12},{12,8},{16,20},{20,16},{24,28},{28,24},{32,36},... | collective-permute-start | bytes 786440 | tf_op jit(solution)/shard_map/ppermute | solution.py:413
  14.9 1.9 %collective-permute-start.1 = (bf16[16,8192]{1,0:T(8,128)(2,1)S(1)}, bf16[16,8192]{1,0:T(8,128)(2,1)S(1)}, u32[]{:S(2)}, u32[]{:S(2)}) collective-permute-start(bf16[16,8192]{1,0:T(8,128)(2,1)S(1)} %get-tuple-element.16), channel_id=1, source_target_pairs={{4,8},{8,4},{12,16},{16,12},{20,24},{24,20},{28,32},{32,28},{36,40... | collective-permute-start | bytes 786440 | tf_op jit(solution)/shard_map/ppermute | solution.py:414
  16.9 12.2 %all-to-all-start = ((bf16[128,4,128]{2,1,0:T(4,128)(2,1)}), bf16[128,4,128]{2,1,0:T(4,128)(2,1)S(1)}, u32[]{:S(2)}, u32[]{:S(2)}) async-start(bf16[128,4,128]{2,1,0:T(4,128)(2,1)} %bitcast.2), calls=%async_computation | async-start | bytes 262144 | tf_op jit(solution)/shard_map/all_to_all | solution.py:410
  29.1 0.0 copy-start
  29.1 1.6 %copy-done = bf16[254,4,32,32]{0,3,2,1:T(8,128)(2,1)S(1)} copy-done((bf16[254,4,32,32]{0,3,2,1:T(8,128)(2,1)S(1)}, bf16[254,4,32,32]{0,3,2,1:T(8,128)(2,1)}, u32[]{:S(2)}) %copy-start) | copy-done | bytes 2080792
  30.7 0.0 copy-start.4
  30.7 1.0 %copy-done.4 = bf16[254,32,32]{0,2,1:T(8,128)(2,1)S(1)} copy-done((bf16[254,32,32]{0,2,1:T(8,128)(2,1)S(1)}, bf16[254,32,32]{0,2,1:T(8,128)(2,1)}, u32[]{:S(2)}) %copy-start.4) | copy-done | bytes 520216
  31.7 0.0 copy-start.9
  31.7 0.7 %copy-done.9 = s32[254,4]{0,1:T(4,128)S(1)} copy-done((s32[254,4]{0,1:T(4,128)S(1)}, s32[254,4]{0,1:T(4,128)}, u32[]{:S(2)}) %copy-start.9) | copy-done | bytes 4088
  32.4 4.2 %operator.1.operator_ref = bf16[32,32,128]{2,1,0:T(8,128)(2,1)S(1)} custom-call(s32[1]{0:T(128)} %bitcast.place_ref, s32[4,254]{1,0:T(4,128)S(1)} %bitcast.15, bf16[32,32,254]{2,1,0:T(8,128)(2,1)S(1)} %bitcast.12, bf16[4,32,32,254]{3,2,1,0:T(8,128)(2,1)S(1)} %bitcast.10, bf16[32,32,128]{2,1,0:T(8,128)(2,1)S(1)} %get-tuple-element.13.order_ref.chunks_ref), custom_call_target="tpu_custom_call" | custom-call | tf_op jit(solution)/shard_map/operator/pallas_call | solution.py:415
  36.6 0.0 collective-permute-done.first_ref
  36.6 0.0 collective-permute-done.1.second_ref
  36.6 0.0 copy-done.10
  36.7 0.0 copy-done.6
  36.7 10.7 %near.1.near_ref = f32[16,4096]{1,0:T(8,128)S(1)} custom-call(s32[1]{0:T(128)} %bitcast.place_ref, s32[8,64]{1,0:T(8,128)S(1)} %bitcast.16, bf16[16,4096]{1,0:T(8,128)(2,1)S(1)} %copy-done.6, bf16[16,4096]{1,0:T(8,128)(2,1)S(1)} %get-tuple-element.14.aug_ref, bf16[16,8192]{1,0:T(8,128)(2,1)S(1)} %collective-permute-done.first_ref, ...), custom_call_target="tpu_custom_call" | custom-call | tf_op jit(solution)/shard_map/near/pallas_call | solution.py:416
  47.4 0.0 copy-done.2
  47.4 0.0 copy-done.3
  47.4 0.0 copy-done.11
  47.4 7.0 %far.1 = (f32[16,4096]{1,0:T(8,128)S(1)}, bf16[32,4096]{1,0:T(8,128)(2,1)S(1)}) custom-call(s32[1]{0:T(128)} %bitcast.place_ref, s32[4,126]{1,0:T(4,128)S(1)} %bitcast.17, bf16[4,32,32,126]{3,2,1,0:T(8,128)(2,1)S(1)} %bitcast.11, bf16[32,32,128]{2,1,0:T(8,128)(2,1)S(1)} %get-tuple-element.13.order_ref.chunks_ref, bf16[32,4096]{1,0:T(8,128)(2,1)S(1)} %copy-done.2, ...), custom_call_target="tpu_custom_call" | custom-call | tf_op jit(solution)/shard_map/far/pallas_call | solution.py:417
  54.5 0.0 all-to-all-done
  54.5 1.1 %final.1 = bf16[16,4096]{1,0:T(8,128)(2,1)} custom-call(bf16[512,128]{1,0:T(8,128)(2,1)S(1)} %bitcast.13, bf16[32,32,128]{2,1,0:T(8,128)(2,1)S(1)} %operator.1.operator_ref, bf16[32,4096]{1,0:T(8,128)(2,1)S(1)} %get-tuple-element.17.basis_ref, f32[16,4096]{1,0:T(8,128)S(1)} %get-tuple-element.18.base_ref), custom_call_target="tpu_custom_call" | custom-call | tf_op jit(solution)/shard_map/final/pallas_call | solution.py:418
  (3 shorter events, 0.0 us)
Async XLA Ops:
  0.0 36.6 %copy-start.10 = (s32[64,8]{0,1:T(8,128)S(1)}, s32[64,8]{0,1:T(8,128)}, u32[]{:S(2)}) copy-start(s32[64,8]{0,1:T(8,128)} %param.17) | copy-start | bytes 6148
  0.0 1.0 %copy-start.1 = (bf16[32,4096]{1,0:T(8,128)(2,1)S(1)}, bf16[32,4096]{1,0:T(8,128)(2,1)}, u32[]{:S(2)}) copy-start(bf16[32,4096]{1,0:T(8,128)(2,1)} %basis_ref.3) | copy-start | bytes 786436
  1.0 0.9 %copy-start.5 = (bf16[16,4096]{1,0:T(8,128)(2,1)S(1)}, bf16[16,4096]{1,0:T(8,128)(2,1)}, u32[]{:S(2)}) copy-start(bf16[16,4096]{1,0:T(8,128)(2,1)} %values_ref.3) | copy-start | bytes 393220
  1.9 0.9 %copy-start.7 = (bf16[126,32,32]{0,2,1:T(8,128)(2,1)S(1)}, bf16[126,32,32]{0,2,1:T(8,128)(2,1)}, u32[]{:S(2)}) copy-start(bf16[126,32,32]{0,2,1:T(8,128)(2,1)} %param.13) | copy-start | bytes 774148
  2.8 0.8 %copy-start.8 = (bf16[3,4096]{1,0:T(4,128)(2,1)S(1)}, bf16[3,4096]{1,0:T(4,128)(2,1)}, u32[]{:S(2)}) copy-start(bf16[3,4096]{1,0:T(4,128)(2,1)} %points_ref.1) | copy-start | bytes 73732
  3.6 33.1 %copy-start.6 = (bf16[16,4096]{1,0:T(8,128)(2,1)S(1)}, bf16[16,4096]{1,0:T(8,128)(2,1)}, u32[]{:S(2)}) copy-start(bf16[16,4096]{1,0:T(8,128)(2,1)} %values_ref.3) | copy-start | bytes 393220
  6.2 30.4 %collective-permute-start = (bf16[16,8192]{1,0:T(8,128)(2,1)S(1)}, bf16[16,8192]{1,0:T(8,128)(2,1)S(1)}, u32[]{:S(2)}, u32[]{:S(2)}) collective-permute-start(bf16[16,8192]{1,0:T(8,128)(2,1)S(1)} %get-tuple-element.15.own_ref), channel_id=1, source_target_pairs={{0,4},{4,0},{8,12},{12,8},{16,20},{20,16},{24,28},{28,24},{32,36},... | collective-permute-start | bytes 786440 | tf_op jit(solution)/shard_map/ppermute | solution.py:413
  14.9 21.7 %collective-permute-start.1 = (bf16[16,8192]{1,0:T(8,128)(2,1)S(1)}, bf16[16,8192]{1,0:T(8,128)(2,1)S(1)}, u32[]{:S(2)}, u32[]{:S(2)}) collective-permute-start(bf16[16,8192]{1,0:T(8,128)(2,1)S(1)} %get-tuple-element.16), channel_id=1, source_target_pairs={{4,8},{8,4},{12,16},{16,12},{20,24},{24,20},{28,32},{32,28},{36,40... | collective-permute-start | bytes 786440 | tf_op jit(solution)/shard_map/ppermute | solution.py:414
  16.9 37.6 %all-to-all-start = ((bf16[128,4,128]{2,1,0:T(4,128)(2,1)}), bf16[128,4,128]{2,1,0:T(4,128)(2,1)S(1)}, u32[]{:S(2)}, u32[]{:S(2)}) async-start(bf16[128,4,128]{2,1,0:T(4,128)(2,1)} %bitcast.2), calls=%async_computation | async-start | bytes 262144 | tf_op jit(solution)/shard_map/all_to_all | solution.py:410
  29.1 1.6 %copy-start = (bf16[254,4,32,32]{0,3,2,1:T(8,128)(2,1)S(1)}, bf16[254,4,32,32]{0,3,2,1:T(8,128)(2,1)}, u32[]{:S(2)}) copy-start(bf16[254,4,32,32]{0,3,2,1:T(8,128)(2,1)} %param.16) | copy-start | bytes 6242308
  30.7 1.0 %copy-start.4 = (bf16[254,32,32]{0,2,1:T(8,128)(2,1)S(1)}, bf16[254,32,32]{0,2,1:T(8,128)(2,1)}, u32[]{:S(2)}) copy-start(bf16[254,32,32]{0,2,1:T(8,128)(2,1)} %param.14) | copy-start | bytes 1560580
  31.7 0.7 %copy-start.9 = (s32[254,4]{0,1:T(4,128)S(1)}, s32[254,4]{0,1:T(4,128)}, u32[]{:S(2)}) copy-start(s32[254,4]{0,1:T(4,128)} %param.19) | copy-start | bytes 12196
  32.4 15.0 %copy-start.2 = (bf16[32,4096]{1,0:T(8,128)(2,1)S(1)}, bf16[32,4096]{1,0:T(8,128)(2,1)}, u32[]{:S(2)}) copy-start(bf16[32,4096]{1,0:T(8,128)(2,1)} %basis_ref.3) | copy-start | bytes 786436
  32.4 15.0 %copy-start.3 = (bf16[126,4,32,32]{0,3,2,1:T(8,128)(2,1)S(1)}, bf16[126,4,32,32]{0,3,2,1:T(8,128)(2,1)}, u32[]{:S(2)}) copy-start(bf16[126,4,32,32]{0,3,2,1:T(8,128)(2,1)} %param.15) | copy-start | bytes 3096580
  32.4 15.0 %copy-start.11 = (s32[126,4]{0,1:T(4,128)S(1)}, s32[126,4]{0,1:T(4,128)}, u32[]{:S(2)}) copy-start(s32[126,4]{0,1:T(4,128)} %param.18) | copy-start | bytes 6052
where the time goes:
time: 56.1 us; the launch traced here: 55.6 us
  Pallas kernels  25.7 us (46%)
  starting transfers between devices  22.9 us (41%)
  local copies, waits for them, and re-layouts  6.94 us (12%)
    all_to_all x1, starting transfers between devices, shards(): roots = lax.all_to_all(root.reshape(GROUP, 4, 128), 'pts', 0, 0, tiled=True)  12.2 us
    pallas_call x1, Pallas kernels, shards(): near_field, = near(place, near_list.T, values, aug, first_in, second_in)  10.7 us
    ppermute x1, starting transfers between devices, shards(): first_in = lax.ppermute(first, 'pts', inside)  8.73 us
    pallas_call x1, Pallas kernels, shards(): far(place, local_partners.T, local_c, chunks, leaf_basis, near_field, fir...  7.05 us
    unnamed x24, local copies, waits for them, and re-layouts  6.94 us
    pallas_call x1, Pallas kernels, shards(): op, = operator(place, upper_partners.T, upper_t, upper_c, chunks)  4.18 us
    pallas_call x1, Pallas kernels, shards(): up(place, values, points, leaf_basis, local_t)  2.6 us
    ppermute x1, starting transfers between devices, shards(): second_in = lax.ppermute(second, 'pts', across)  1.92 us
  transfers between devices with their start and end apart: 3, of which 0 were waited for; matrix products, arithmetic and copies ran while one was open for 0% of the time, Pallas kernels for 39%

commit v1 on v0

v1 whole, which is shorter than its diff:
```python
import functools

import jax
import jax.numpy as jnp
from jax import lax
from jax.experimental import pallas as pl
from jax.experimental.pallas import tpu as pltpu
from jax.sharding import PartitionSpec as P

BF = jnp.bfloat16
F32 = jnp.float32
COLS = 16
RANK = 32
POINTS = 4096
HALF = POINTS // 2
GROUP = 128

PITCH = RANK + 1
LEAVES_PER_STEP = 8

LOCAL_BASE = (0, 16, 24, 28, 30, 31)
UPPER_BASE = (0, 32, 48, 56, 60, 62, 63)


def _dot(a, b, ca, cb):
    return lax.dot_general(a, b, (((ca,), (cb,)), ((), ())), preferred_element_type=F32)


def nn(a, b):
    return _dot(a, b, 1, 0)


def nt(a, b):
    return _dot(a, b, 1, 1)


def iota(shape, dim):
    return lax.broadcasted_iota(jnp.int32, shape, dim)


def ones_where(cond):
    return jnp.where(cond, F32(1), F32(0)).astype(BF)


def pair_mask():
    shape = (128, 256)
    return ones_where(iota(shape, 0) // 32 == iota(shape, 1) // 64)


def spread_mask():
    shape = (128, 512)
    row, col = iota(shape, 0), iota(shape, 1)
    return ones_where((row // 32 == col // 128) & (row % 32 == col % 32))


def tile_rows(x):
    return jnp.concatenate([x, x, x, x], axis=0)


def to_chunks(matrix_ref, chunk_ref, count, chunks):
    keep = ones_where(iota((128, count), 1) % 4 == iota((128, count), 0) // 32)
    pick = ones_where(iota((chunks, count), 1) // 4 == iota((chunks, count), 0))
    for r in range(RANK):
        part = tile_rows(matrix_ref[r]) * keep
        chunk_ref[pl.ds(r, chunks, stride=PITCH), :] = nt(pick, part)


def chunk_of(ref, index):
    return ref[index * PITCH : index * PITCH + RANK, :].astype(BF)


def fetch_all(pairs, sems):
    copies = [pltpu.make_async_copy(a, b, sems.at[i]) for i, (a, b) in enumerate(pairs)]
    for copy in copies:
        copy.start()
    return copies


def up_kernel(
    place_ref, values_in, points_in, basis_in, transfer_in,
    first_ref, second_ref, aug_ref, root_ref, chunks_ref,
    values_ref, basis_ref, points_ref, transfer_ref, scratch_ref, sems,
):
    pairs = (
        (transfer_in, transfer_ref), (values_in, values_ref), (basis_in, basis_ref), (points_in, points_ref),
    )
    copies = fetch_all(pairs, sems)
    mask = pair_mask()
    copies[0].wait()
    to_chunks(transfer_ref, scratch_ref, 126, 32)
    blocks = [chunk_of(scratch_ref, i) for i in range(32)]
    for i in range(32):
        chunks_ref[i] = blocks[i]
    copies[1].wait()
    copies[2].wait()
    upward = []
    for g in range(16):
        lanes = slice(g * 256, (g + 1) * 256)
        weights = tile_rows(basis_ref[:, lanes]) * mask
        upward.append(nt(values_ref[:, lanes], weights).astype(BF))
    for base, below in ((16, 0), (24, 16), (28, 24), (30, 28)):
        for j in range((base - below) // 2):
            c = below + 2 * j
            weights = tile_rows(jnp.concatenate([blocks[c], blocks[c + 1]], axis=1)) * mask
            children = jnp.concatenate([upward[c], upward[c + 1]], axis=1)
            upward.append(nt(children, weights).astype(BF))
    upward.append(nt(upward[30], tile_rows(blocks[30]) * mask[:, :128]).astype(BF))
    root = nt(upward[31], tile_rows(blocks[31])).astype(BF).astype(F32)
    shape = (COLS, 128)
    root = jnp.where(iota(shape, 0) // 4 == iota(shape, 1) // 32, root, 0.0)
    root = root[:8] + root[8:]
    root = jnp.concatenate([root[:4] + root[4:]] * 2, axis=0).astype(BF)
    for i in range(64):
        root_ref[i * 8 : (i + 1) * 8, :] = root

    copies[3].wait()
    for g in range(8):
        lanes = slice(g * 512, (g + 1) * 512)
        coords = points_ref[:, lanes].astype(F32)
        square = coords * coords
        square = square[0:1] + square[1:2] + square[2:3]
        high = square.astype(BF).astype(F32)
        middle = (square - high).astype(BF).astype(F32)
        low = (square - high - middle).astype(BF).astype(F32)
        row = iota((8, 512), 0)
        top = jnp.where(row == 0, coords[0:1], jnp.where(row == 1, coords[1:2], coords[2:3]))
        top = jnp.where(row < 3, top, jnp.where(row < 6, 1.0, jnp.where(row == 6, -high, -middle)))
        bottom = jnp.where(row == 0, -low, 0.0)
        aug_ref[:, lanes] = jnp.concatenate([top, bottom], axis=0).astype(BF)

    odd = lax.rem(place_ref[0], 2)
    for ref, start in ((first_ref, (1 - odd) * HALF), (second_ref, odd * HALF)):
        start = pl.multiple_of(start, HALF)
        ref[:, 0:HALF] = values_ref[:, pl.ds(start, HALF)]
        ref[:, HALF : 2 * HALF] = aug_ref[:, pl.ds(start, HALF)]
        for i in range(32):
            ref[:, 2 * HALF + i * 128 : 2 * HALF + (i + 1) * 128] = upward[i]


def operator_part(
    place, partners_ref, transfer_ref, coupling_ref, out_ref, blocks_ref, near_ref, spread_ref, weights_ref, waits,
):
    mask = pair_mask()
    waits[0].wait()
    to_chunks(transfer_ref, blocks_ref, 254, 64)
    level = iota((8, 254), 0)
    mine = 256 - (256 >> level) + (place >> level)
    chosen = ones_where((iota((8, 254), 1) == mine) & (level < 7))
    waits[1].wait()
    for r in range(RANK):
        part = jnp.concatenate([coupling_ref[f, r] for f in range(4)], axis=0)
        near_ref[pl.ds(r, 8, stride=PITCH), :] = nt(chosen, part)
    lane_group = iota((RANK, 128), 1) // 32
    chain = ones_where(iota((RANK, 128), 0) == iota((RANK, 128), 1) % 32)
    direct = []
    for k in range(7):
        direct.append(nn(chain[:, :RANK], chunk_of(near_ref, k)).astype(BF))
        if k < 6:
            own = place >> k
            block = blocks_ref[pl.ds((UPPER_BASE[k] + (own >> 2)) * PITCH, RANK), :]
            block = jnp.where(lane_group == (own & 3), block, 0.0).astype(BF)
            chain = nt(chain, tile_rows(block)).astype(BF)
    spread_ref[...] = nn(jnp.concatenate(direct, axis=0), spread_mask())
    weights_ref[...] = jnp.zeros_like(weights_ref)
    waits[2].wait()
    for k in range(7):
        row = 256 - (256 >> k) + (place >> k)
        for f in range(4):
            partner = partners_ref[f, row]
            found = jnp.maximum(partner, 0)
            at = pl.multiple_of((UPPER_BASE[k] + (found >> 2)) * RANK, RANK)
            group = jnp.where(partner < 0, -1, found & 3)
            term = spread_ref[k * RANK : (k + 1) * RANK, f * 128 : (f + 1) * 128]
            old = weights_ref[pl.ds(at, RANK), :]
            weights_ref[pl.ds(at, RANK), :] = old + jnp.where(lane_group == group, term, 0.0)
    held = {63: weights_ref[63 * RANK : 64 * RANK, :].astype(BF)}
    step = nn(held[63], tile_rows(chunk_of(blocks_ref, 62)) * mask[:, :128])
    held[62] = (weights_ref[62 * RANK : 63 * RANK, :] + step).astype(BF)
    for k in (4, 3, 2, 1, 0):
        for j in range((UPPER_BASE[k + 1] - UPPER_BASE[k]) // 2):
            c = UPPER_BASE[k] + 2 * j
            pair = jnp.concatenate([chunk_of(blocks_ref, c), chunk_of(blocks_ref, c + 1)], axis=1)
            step = nn(held[UPPER_BASE[k + 1] + j], tile_rows(pair) * mask)
            for h in range(2):
                total = weights_ref[(c + h) * RANK : (c + h + 1) * RANK, :]
                held[c + h] = (total + step[:, h * 128 : (h + 1) * 128]).astype(BF)
    for c in range(32):
        out_ref[c] = held[c]


def near_part(
    place, list_ref, values_ref, aug_ref, first_ref, second_ref, near_ref, low_ref, high_ref, target_ref, waits,
):
    waits[0].wait()
    odd = lax.rem(place, 2)
    lane = iota((32, 128), 1)
    in_low, in_high = ones_where(lane < 64), ones_where(lane >= 64)

    def stage(ref, first_leaf, value_at, aug_source, aug_at):
        for i in range(16):
            block = jnp.concatenate(
                [
                    ref[:, value_at + i * 128 : value_at + (i + 1) * 128],
                    aug_source[:, aug_at + i * 128 : aug_at + (i + 1) * 128],
                ],
                axis=0,
            )
            turned = pltpu.roll(block.astype(F32), 64, 1).astype(BF)
            low_ref[first_leaf + 2 * i] = block * in_low
            high_ref[first_leaf + 2 * i] = turned * in_high
            low_ref[first_leaf + 2 * i + 1] = turned * in_low
            high_ref[first_leaf + 2 * i + 1] = block * in_high

    stage(values_ref, 32, 0, aug_ref, 0)
    stage(values_ref, 64, HALF, aug_ref, HALF)
    stage(first_ref, (1 - odd) * 96, 0, first_ref, HALF)
    stage(second_ref, odd * 96, 0, second_ref, HALF)
    low_ref[128] = jnp.zeros((32, 128), BF)
    high_ref[128] = jnp.zeros((32, 128), BF)

    row, col = iota((16, 16), 0), iota((16, 16), 1)
    swap = jnp.where(
        (row < 3) & (row == col), 2.0,
        jnp.where((row >= 3) & (col >= 3) & (row < 9) & (col < 9) & ((row + 3 == col) | (row == col + 3)), 1.0, 0.0),
    ).astype(BF)
    for i in range(32):
        lanes = slice(i * 128, (i + 1) * 128)
        target_ref[lanes, :] = _dot(aug_ref[:, lanes], swap, 0, 0).astype(BF)

    base = place * 64 - 32
    waits[1].wait()

    def step(m, carry):
        stacks = []
        for h in range(LEAVES_PER_STEP):
            leaf = LEAVES_PER_STEP * m + h
            columns = []
            for f in range(0, 8, 2):
                left, right = list_ref[f, leaf], list_ref[f + 1, leaf]
                left = jnp.where(left < 0, 128, left - base)
                right = jnp.where(right < 0, 128, right - base)
                columns.append(low_ref[left] + high_ref[right])
            stacks.append(jnp.concatenate(columns, axis=1))
        kernel = []
        for h in range(LEAVES_PER_STEP):
            leaf = LEAVES_PER_STEP * m + h
            targets = target_ref[pl.ds(pl.multiple_of(leaf * 64, 64), 64), :]
            kernel.append(jnp.exp(nn(targets, stacks[h][16:])).astype(BF))
        results = [nt(stacks[h][:16], kernel[h]) for h in range(LEAVES_PER_STEP)]
        width = 64 * LEAVES_PER_STEP
        near_ref[:, pl.ds(pl.multiple_of(m * width, width), width)] = jnp.concatenate(results, axis=1)
        return carry

    lax.fori_loop(0, 64 // LEAVES_PER_STEP, step, 0)


def far_part(
    place, partners_ref, coupling_ref, chunks_ref, basis_ref, own_ref, first_ref, second_ref,
    base_ref, basis_out_ref, blocks_ref, spread_ref, coupled_ref, waits,
):
    waits[0].wait()
    odd = lax.rem(place, 2)
    same = ones_where(iota((128, 126), 0) == iota((128, 126), 1))
    for r in range(RANK):
        part = jnp.concatenate([coupling_ref[f, r] for f in range(4)], axis=0)
        blocks_ref[pl.ds(r, 128, stride=PITCH), :] = nt(same, part)
    spread = spread_mask()
    for ref, piece in ((own_ref, 1), (first_ref, (1 - odd) * 2), (second_ref, odd * 2)):
        rows = [ref[:, POINTS + i * 128 : POINTS + (i + 1) * 128] for i in range(32)]
        out = nn(jnp.concatenate(rows, axis=0), spread).astype(BF)
        for height in range(6):
            clusters = 64 >> height
            offset = 128 - 2 * clusters
            first = 3 * offset + piece * clusters
            for j in range(clusters):
                i, group = divmod(offset + j, 4)
                block = out[i * COLS : (i + 1) * COLS, group * 128 : (group + 1) * 128]
                spread_ref[first + j] = block
    spread_ref[384] = jnp.zeros((COLS, 128), BF)
    waits[1].wait()

    group = iota((COLS, 128), 1) // 32
    slot_masks = [ones_where(group == f) for f in range(4)]
    zero = jnp.zeros((RANK, 128), BF)
    nothing = jnp.zeros((COLS, 128), BF)

    def couple(chunk, height, live):
        base = 3 * (128 - (128 >> height)) - ((place - 1) << (6 - height))
        lefts, rights = [], []
        for j in range(4):
            if j >= live:
                lefts.append(nothing)
                rights.append(jnp.concatenate([zero] * 4, axis=1))
                continue
            total = nothing
            for f in range(4):
                partner = partners_ref[f, chunk * 4 + j]
                at = jnp.where(partner < 0, 384, partner + base)
                total = total + spread_ref[at] * slot_masks[f]
            lefts.append(total)
            block = blocks_ref[pl.ds((chunk * 4 + j) * PITCH, RANK), :].astype(BF)
            rights.append(jnp.concatenate([zero] * j + [block] + [zero] * (3 - j), axis=1))
        result = nt(jnp.concatenate(lefts, axis=1), jnp.concatenate(rights, axis=0))
        coupled_ref[pl.ds(pl.multiple_of(chunk * COLS, COLS), COLS), :] = result

    for height in range(6):
        first = LOCAL_BASE[height]
        count = 16 >> height if height < 5 else 1
        if count >= 4:
            lax.fori_loop(0, count, lambda i, c, f=first, h=height: (couple(f + i, h, 4), c)[1], 0, unroll=2)
        else:
            for i in range(count):
                couple(first + i, height, 4 if height < 5 else 2)

    waits[2].wait()
    mask = pair_mask()
    pad = jnp.zeros((RANK, 128), F32)

    def coupled(c):
        return coupled_ref[c * COLS : (c + 1) * COLS, :]

    held = {31: jnp.concatenate([coupled(31).astype(BF), chunks_ref[31]], axis=0)}
    step = nn(held[31], tile_rows(chunks_ref[30]) * mask[:, :128])
    held[30] = (step + jnp.concatenate([coupled(30), pad], axis=0)).astype(BF)
    for height in (3, 2, 1, 0):
        for j in range((LOCAL_BASE[height + 1] - LOCAL_BASE[height]) // 2):
            c = LOCAL_BASE[height] + 2 * j
            pair = jnp.concatenate([chunks_ref[c], chunks_ref[c + 1]], axis=1)
            step = nn(held[LOCAL_BASE[height + 1] + j], tile_rows(pair) * mask)
            for h in range(2):
                extra = jnp.concatenate([coupled(c + h), pad], axis=0)
                held[c + h] = (step[:, h * 128 : (h + 1) * 128] + extra).astype(BF)
    for g in range(16):
        lanes = slice(g * 256, (g + 1) * 256)
        out = nn(held[g], tile_rows(basis_ref[:, lanes]) * mask)
        base_ref[:, lanes] += out[:COLS]
        basis_out_ref[:, lanes] = out[COLS:].astype(BF)


def main_kernel(
    place_ref, upper_partners_in, partners_in, list_in, upper_transfer_in, upper_coupling_in, coupling_in, values_in,
    basis_in, aug_ref, chunks_ref, own_ref, first_ref, second_ref,
    operator_ref, base_ref, basis_out_ref,
    upper_partners_ref, partners_ref, list_ref, upper_transfer_ref, upper_coupling_ref, coupling_ref, values_ref,
    basis_ref, upper_blocks_ref, picked_ref, terms_ref, weights_ref, low_ref, high_ref, target_ref, blocks_ref,
    spread_ref, coupled_ref, sems,
):
    pairs = (
        (upper_transfer_in, upper_transfer_ref), (upper_coupling_in, upper_coupling_ref),
        (upper_partners_in, upper_partners_ref), (values_in, values_ref), (list_in, list_ref),
        (coupling_in, coupling_ref), (partners_in, partners_ref), (basis_in, basis_ref),
    )
    copies = fetch_all(pairs, sems)
    place = place_ref[0]
    operator_part(
        place, upper_partners_ref, upper_transfer_ref, upper_coupling_ref, operator_ref, upper_blocks_ref,
        picked_ref, terms_ref, weights_ref, copies[0:3],
    )
    near_part(
        place, list_ref, values_ref, aug_ref, first_ref, second_ref, base_ref, low_ref, high_ref, target_ref,
        copies[3:5],
    )
    far_part(
        place, partners_ref, coupling_ref, chunks_ref, basis_ref, own_ref, first_ref, second_ref, base_ref,
        basis_out_ref, blocks_ref, spread_ref, coupled_ref, copies[5:8],
    )


def final_kernel(roots_ref, operator_ref, basis_ref, base_ref, out_ref):
    roots = roots_ref[...].astype(F32)
    roots = roots.reshape(32, COLS, 128)
    shape = (32, COLS, 128)
    device, column = iota(shape, 2) // 32, iota(shape, 1) // 4
    total = jnp.where(device == column, roots, 0.0)
    for d in range(1, 4):
        moved = pltpu.roll(pltpu.roll(roots, COLS - 4 * d, 1), 32 * d, 2)
        total = jnp.where(device == (column + d) % 4, moved, total)
    total = total.astype(BF)
    left = jnp.concatenate([total[i] for i in range(32)], axis=1)
    right = jnp.concatenate([operator_ref[i] for i in range(32)], axis=1)
    expansion = nt(left, right).astype(BF)
    for g in range(8):
        lanes = slice(g * 512, (g + 1) * 512)
        out_ref[:, lanes] = (base_ref[:, lanes] + nn(expansion, basis_ref[:, lanes])).astype(BF)


SMEM = pl.BlockSpec(memory_space=pltpu.SMEM)
VMEM = pl.BlockSpec(memory_space=pltpu.VMEM)
HBM = pl.BlockSpec(memory_space=pltpu.HBM)
SCRATCH = pltpu.VMEM
DMA = pltpu.SemaphoreType.DMA


def call(kernel, ins, outs, scratch, name, interpret=False):
    return pl.pallas_call(
        kernel,
        in_specs=ins,
        out_specs=[VMEM] * len(outs),
        out_shape=[jax.ShapeDtypeStruct(s, d) for s, d in outs],
        scratch_shapes=scratch,
        compiler_params=pltpu.CompilerParams(vmem_limit_bytes=32 * 1024 * 1024),
        name=name,
        interpret=interpret,
    )


def kernels(interpret=False):
    up = call(
        up_kernel,
        [SMEM] + [HBM] * 4,
        [
            ((COLS, 2 * POINTS), BF),
            ((COLS, 2 * POINTS), BF),
            ((16, POINTS), BF),
            ((4 * GROUP, 128), BF),
            ((32, RANK, 128), BF),
        ],
        [
            SCRATCH((COLS, POINTS), BF),
            SCRATCH((RANK, POINTS), BF),
            SCRATCH((3, POINTS), BF),
            SCRATCH((RANK, RANK, 126), BF),
            SCRATCH((32 * PITCH, 128), F32),
            DMA((4,)),
        ],
        "up",
        interpret,
    )
    main = call(
        main_kernel,
        [SMEM] + [HBM] * 8 + [VMEM] * 5,
        [((32, RANK, 128), BF), ((COLS, POINTS), F32), ((RANK, POINTS), BF)],
        [
            pltpu.SMEM((4, 254), jnp.int32),
            pltpu.SMEM((4, 126), jnp.int32),
            pltpu.SMEM((8, 64), jnp.int32),
            SCRATCH((RANK, RANK, 254), BF),
            SCRATCH((4, RANK, RANK, 254), BF),
            SCRATCH((4, RANK, RANK, 126), BF),
            SCRATCH((COLS, POINTS), BF),
            SCRATCH((RANK, POINTS), BF),
            SCRATCH((64 * PITCH, 128), F32),
            SCRATCH((8 * PITCH, 128), F32),
            SCRATCH((7 * RANK, 512), F32),
            SCRATCH((64 * RANK, 128), F32),
            SCRATCH((129, 32, 128), BF),
            SCRATCH((129, 32, 128), BF),
            SCRATCH((POINTS, 16), BF),
            SCRATCH((128 * PITCH, 128), F32),
            SCRATCH((385, COLS, 128), BF),
            SCRATCH((32 * COLS, 128), F32),
            DMA((8,)),
        ],
        "main",
        interpret,
    )
    final = call(final_kernel, [VMEM] * 4, [((COLS, POINTS), BF)], [], "final", interpret)
    return up, main, final


def shards(
    points, values, leaf_basis, local_transfer, upper_transfer, local_coupling, upper_coupling,
    near_list, local_partners, upper_partners,
):
    up, main, final = kernels()
    place = lax.axis_index("pts").astype(jnp.int32).reshape(1)
    local_t = jnp.transpose(local_transfer, (1, 2, 0))
    upper_t = jnp.transpose(upper_transfer, (1, 2, 0))
    local_c = jnp.transpose(local_coupling, (1, 2, 3, 0))
    upper_c = jnp.transpose(upper_coupling, (1, 2, 3, 0))
    values, points, leaf_basis, local_t, upper_t, upper_c, local_c, near_list, local_partners, upper_partners = (
        pltpu.with_memory_space_constraint(x, pltpu.HBM)
        for x in (
            values, points, leaf_basis, local_t, upper_t, upper_c, local_c, near_list.T, local_partners.T, upper_partners.T
        )
    )
    first, second, aug, root, chunks = up(place, values, points, leaf_basis, local_t)
    roots = lax.all_to_all(root.reshape(GROUP, 4, 128), "pts", 0, 0, tiled=True)
    inside = [(i, i ^ 1) for i in range(GROUP)]
    across = [(i, ((i + 1) ^ 1) - 1) for i in range(1, GROUP - 1)]
    first_in = lax.ppermute(first, "pts", inside)
    second_in = lax.ppermute(second, "pts", across)
    op, base, basis = main(
        place, upper_partners, local_partners, near_list, upper_t, upper_c, local_c, values, leaf_basis,
        aug, chunks, first, first_in, second_in,
    )
    (out,) = final(roots.reshape(4 * GROUP, 128), op, basis, base)
    return out


def solution(mesh):
    placed = (
        P(None, "pts"),
        P("rhs", "pts"),
        P(None, "pts"),
        P("pts", None, None),
        P(),
        P("pts", None, None, None),
        P(),
        P("pts", None),
        P("pts", None),
        P(),
    )
    return jax.shard_map(
        shards, mesh=mesh, in_specs=placed, out_specs=P("rhs", "pts"), check_vma=False
    )
```

time: 56.1 us -> 42.3 us (0.75)
  local copies, waits for them, and re-layouts: 6.94 us -> 0 us
  Pallas kernels: 25.7 us -> 19 us
    pallas_call x3 -> x1, Pallas kernels: 21.9 us -> 14.4 us  [shards(): main(place, upper_partners, local_partners, near_list, upper_t, upper_c,...]
    unnamed x24 -> x0, local copies, waits for them, and re-layouts: 6.94 us -> none
    ppermute x1, starting transfers between devices: 8.73 us -> 4.84 us  [shards(): first_in = lax.ppermute(first, 'pts', inside)]
    ppermute x1, starting transfers between devices: 1.92 us -> 4.58 us  [shards(): second_in = lax.ppermute(second, 'pts', across)]
    all_to_all x1, starting transfers between devices: 12.2 us -> 13.6 us  [shards(): roots = lax.all_to_all(root.reshape(GROUP, 4, 128), 'pts', 0, 0, tiled=True)]
    pallas_call x1, Pallas kernels: 2.6 us -> 3.46 us  [shards(): up(place, values, points, leaf_basis, local_t)]
  transfers between devices with their start and end apart: 3 -> 3, of which waited for: 0 -> 0; matrix products, arithmetic and copies ran while one was open for 0% -> 0% of each run, Pallas kernels for 39% -> 34%
where the time goes in v1:
time: 42.3 us; the launch traced here: 42.1 us
  starting transfers between devices  23 us (54%)
  Pallas kernels  19 us (45%)
    pallas_call x1, Pallas kernels, shards(): main(place, upper_partners, local_partners, near_list, upper_t, upper_c,...  14.4 us
    all_to_all x1, starting transfers between devices, shards(): roots = lax.all_to_all(root.reshape(GROUP, 4, 128), 'pts', 0, 0, tiled=True)  13.6 us
    ppermute x1, starting transfers between devices, shards(): first_in = lax.ppermute(first, 'pts', inside)  4.84 us
    ppermute x1, starting transfers between devices, shards(): second_in = lax.ppermute(second, 'pts', across)  4.58 us
    pallas_call x1, Pallas kernels, shards(): up(place, values, points, leaf_basis, local_t)  3.46 us
    pallas_call x1, Pallas kernels, shards(): out, = final(roots.reshape(4 * GROUP, 128), op, basis, base)  1.13 us
  transfers between devices with their start and end apart: 3, of which 0 were waited for; matrix products, arithmetic and copies ran while one was open for 0% of the time, Pallas kernels for 34%

profile of v1, /device:TPU:1, one launch (start us, length us, event | category | flops | bytes accessed | tf_op | source)
XLA Modules:
  0.0 42.1 jit_solution(5722605520143802804)
XLA Ops:
  0.0 3.5 %up.1 = (bf16[16,8192]{1,0:T(8,128)(2,1)S(1)}, bf16[16,8192]{1,0:T(8,128)(2,1)S(1)}, bf16[16,4096]{1,0:T(8,128)(2,1)S(1)}, bf16[512,128]{1,0:T(8,128)(2,1)}, bf16[32,32,128]{2,1,0:T(8,128)(2,1)S(1)}) custom-call(s32[1]{0:T(128)} %bitcast.place_ref, bf16[16,4096]{1,0:T(8,128)(2,1)} %values_in.3, bf16[3,4096]{1,0:T(4,128)(2,1)} %points_in.1, ...), custom_call_target="tpu_custom_call" | custom-call | tf_op jit(solution)/shard_map/up/pallas_call | solution.py:477
  3.5 4.6 %collective-permute-start.1 = (bf16[16,8192]{1,0:T(8,128)(2,1)S(1)}, bf16[16,8192]{1,0:T(8,128)(2,1)S(1)}, u32[]{:S(2)}, u32[]{:S(2)}) collective-permute-start(bf16[16,8192]{1,0:T(8,128)(2,1)S(1)} %get-tuple-element.17), channel_id=1, source_target_pairs={{4,8},{8,4},{12,16},{16,12},{20,24},{24,20},{28,32},{32,28},{36,40... | collective-permute-start | bytes 786440 | tf_op jit(solution)/shard_map/ppermute | solution.py:482
  8.1 4.8 %collective-permute-start = (bf16[16,8192]{1,0:T(8,128)(2,1)S(1)}, bf16[16,8192]{1,0:T(8,128)(2,1)S(1)}, u32[]{:S(2)}, u32[]{:S(2)}) collective-permute-start(bf16[16,8192]{1,0:T(8,128)(2,1)S(1)} %get-tuple-element.16.own_ref), channel_id=1, source_target_pairs={{0,4},{4,0},{8,12},{12,8},{16,20},{20,16},{24,28},{28,24},{32,36},... | collective-permute-start | bytes 786440 | tf_op jit(solution)/shard_map/ppermute | solution.py:481
  12.9 13.6 %all-to-all-start = ((bf16[128,4,128]{2,1,0:T(4,128)(2,1)}), bf16[128,4,128]{2,1,0:T(4,128)(2,1)S(1)}, u32[]{:S(2)}, u32[]{:S(2)}) async-start(bf16[128,4,128]{2,1,0:T(4,128)(2,1)} %bitcast.2), calls=%async_computation | async-start | bytes 262144 | tf_op jit(solution)/shard_map/all_to_all | solution.py:478
  26.5 0.0 collective-permute-done.1.second_ref
  26.5 0.0 collective-permute-done.first_ref
  26.5 14.4 %main.1 = (bf16[32,32,128]{2,1,0:T(8,128)(2,1)S(1)}, f32[16,4096]{1,0:T(8,128)S(1)}, bf16[32,4096]{1,0:T(8,128)(2,1)S(1)}) custom-call(s32[1]{0:T(128)} %bitcast.place_ref, s32[4,254]{1,0:T(4,128)} %bitcast.15, s32[4,126]{1,0:T(4,128)} %bitcast.17, s32[8,64]{1,0:T(8,128)} %bitcast.16, bf16[32,32,254]{2,1,0:T(8,128)(2,1)} %bitcast.13, ...), custom_call_target="tpu_custom_call" | custom-call | tf_op jit(solution)/shard_map/main/pallas_call | solution.py:483
  41.0 0.0 all-to-all-done
  41.0 1.1 %final.1 = bf16[16,4096]{1,0:T(8,128)(2,1)} custom-call(bf16[512,128]{1,0:T(8,128)(2,1)S(1)} %bitcast.10, bf16[32,32,128]{2,1,0:T(8,128)(2,1)S(1)} %get-tuple-element.18.operator_ref, bf16[32,4096]{1,0:T(8,128)(2,1)S(1)} %get-tuple-element.19.basis_ref, f32[16,4096]{1,0:T(8,128)S(1)} %get-tuple-element.20.base_ref), custom_call_target="tpu_custom_call" | custom-call | tf_op jit(solution)/shard_map/final/pallas_call | solution.py:487
Async XLA Ops:
  3.5 23.1 %collective-permute-start.1 = (bf16[16,8192]{1,0:T(8,128)(2,1)S(1)}, bf16[16,8192]{1,0:T(8,128)(2,1)S(1)}, u32[]{:S(2)}, u32[]{:S(2)}) collective-permute-start(bf16[16,8192]{1,0:T(8,128)(2,1)S(1)} %get-tuple-element.17), channel_id=1, source_target_pairs={{4,8},{8,4},{12,16},{16,12},{20,24},{24,20},{28,32},{32,28},{36,40... | collective-permute-start | bytes 786440 | tf_op jit(solution)/shard_map/ppermute | solution.py:482
  8.1 18.5 %collective-permute-start = (bf16[16,8192]{1,0:T(8,128)(2,1)S(1)}, bf16[16,8192]{1,0:T(8,128)(2,1)S(1)}, u32[]{:S(2)}, u32[]{:S(2)}) collective-permute-start(bf16[16,8192]{1,0:T(8,128)(2,1)S(1)} %get-tuple-element.16.own_ref), channel_id=1, source_target_pairs={{0,4},{4,0},{8,12},{12,8},{16,20},{20,16},{24,28},{28,24},{32,36},... | collective-permute-start | bytes 786440 | tf_op jit(solution)/shard_map/ppermute | solution.py:481
  12.9 28.1 %all-to-all-start = ((bf16[128,4,128]{2,1,0:T(4,128)(2,1)}), bf16[128,4,128]{2,1,0:T(4,128)(2,1)S(1)}, u32[]{:S(2)}, u32[]{:S(2)}) async-start(bf16[128,4,128]{2,1,0:T(4,128)(2,1)} %bitcast.2), calls=%async_computation | async-start | bytes 262144 | tf_op jit(solution)/shard_map/all_to_all | solution.py:478
